TPU v7x, 128 devices: a whole 4x4x4 slice. The times are simulated.
128 devices in a mesh: sx: 16 (over z, y), sy: 8 (over x, core).
Axes of the slice: x: 4, y: 4, z: 4, core: 2. Of those that a mesh axis runs over, the one named last changes fastest.
Arguments:
- obs_values: bfloat16 [32768, 64], P(('sx', 'sy')), may hold values from -6 to 6
- obs_dest: int32 [32768, 1], P(('sx', 'sy')), may hold values from 0 to 127; in each aligned block of 256 rows (0 to 255, 256 to 511, ...) at most 4 rows name the same one
- obs_node: int32 [32768], P(('sx', 'sy')), may hold values from 0 to 2047
- schur: bfloat16 [16, 8, 2048, 2048], P('sx', 'sy'), as said below
- local_inverse: bfloat16 [16, 8, 2048, 2048], P('sx', 'sy'), as said below
- coarse_inverse: float32 [1024, 1024], P(('sx', 'sy')), as said below
Outputs:
- solution_field: float32 [16, 8, 64, 2048], P('sx', 'sy')
- residual: float32 [16, 8, 64, 2048], P('sx', 'sy')
Inputs may be any that keep to these rules, and one draw needn't show every extreme that they name: `obs_dest`: at most 4 observations of one device go to one subdomain. `schur`: symmetric positive definite. `local_inverse`: symmetric positive definite. `coarse_inverse`: symmetric positive definite.
All inputs are finite; a program needn't handle non-finite values.
Results may differ from a plain program's by a relative error of at most 0.04.
Values may be sent and summed in bfloat16 or wider, within the bound.
A program may use at most 128 MiB of HBM per device.

v0:
```python
import jax
import jax.numpy as jnp
from jax import lax
from jax.sharding import PartitionSpec as P

ITERS = 6


def shortened(array):

    def short(part):
        return part.astype(jnp.bfloat16) if part.dtype == jnp.float32 else part

    return jax.tree.map(short, array)


def padded_2(cells, sides, width):
    for axis, dim in sides:
        count = lax.axis_size(axis)
        ends = count - 1
        head = lax.slice_in_dim(cells, 0, width, axis=dim)
        tail = lax.slice_in_dim(cells, cells.shape[dim] - width, cells.shape[dim], axis=dim)
        cells = jnp.concatenate(
            [
                lax.ppermute(tail, axis, [(i, (i + 1) % count) for i in range(ends)]),
                cells,
                lax.ppermute(head, axis, [((i + 1) % count, i) for i in range(ends)]),
            ],
            axis=dim,
        )
    return cells


def edge_weights(size):
    edge_len = size // 4
    col_index = lax.axis_index("sx")
    row_index = lax.axis_index("sy")
    col_count = lax.axis_size("sx")
    row_count = lax.axis_size("sy")
    sides = (
        jnp.where(col_index > 0, 0.5, 1.0),
        jnp.where(col_index < col_count - 1, 0.5, 1.0),
        jnp.where(row_index > 0, 0.5, 1.0),
        jnp.where(row_index < row_count - 1, 0.5, 1.0),
    )
    return jnp.concatenate([jnp.full((edge_len,), value, jnp.float32) for value in sides])


def coarse_basis(size, count):
    edge_len = size // 4
    node = jnp.arange(size)
    side = node // edge_len
    offset = (node % edge_len).astype(jnp.float32) - (edge_len - 1) / 2.0
    norm_ramp = jnp.sqrt(jnp.float32(edge_len * (edge_len * edge_len - 1) / 12.0))
    column = jnp.arange(count)
    on_edge = side[:, None] == (column // 2)[None, :]
    value = jnp.where(
        (column % 2 == 0)[None, :],
        1.0 / jnp.sqrt(jnp.float32(edge_len)),
        offset[:, None] / norm_ramp,
    )
    return jnp.where(on_edge, value, 0.0)


def assemble(local):
    edge_len = local.shape[1] // 4
    west_part = local[:, 0:edge_len]
    east_part = local[:, edge_len : 2 * edge_len]
    south_part = local[:, 2 * edge_len : 3 * edge_len]
    north_part = local[:, 3 * edge_len :]
    padded = padded_2(shortened(local[None, None]), (("sx", 0), ("sy", 1)), 1)
    west = west_part + padded[0, 1, :, edge_len : 2 * edge_len]
    east = east_part + padded[2, 1, :, 0:edge_len]
    south = south_part + padded[1, 0, :, 3 * edge_len :]
    north = north_part + padded[1, 2, :, 2 * edge_len : 3 * edge_len]
    return jnp.concatenate([west, east, south, north], axis=1)


def gather_coarse(coarse_local):
    return lax.all_gather(coarse_local, ("sx", "sy"), axis=0, tiled=True)


def body(obs_values, obs_dest, obs_node, schur, local_inverse, coarse_inverse):
    hp = lax.Precision.HIGHEST
    size = schur.shape[-1]
    count = coarse_inverse.shape[0]
    realiz = obs_values.shape[1]
    obs_count = obs_values.shape[0]
    row_count = lax.axis_size("sy")
    dev_count = lax.axis_size("sx") * row_count
    target = obs_dest[:, 0]
    capacity = max(2, 2 * obs_count // dev_count)
    match_table = (target[:, None] == jnp.arange(dev_count)[None, :]).astype(jnp.int32)
    slot_index = jnp.sum(jnp.cumsum(match_table, axis=0) * match_table, axis=1) - 1
    position = target * capacity + slot_index
    send_values = (
        jnp.zeros((dev_count * capacity, realiz), jnp.bfloat16).at[position].set(obs_values)
    )
    send_nodes = jnp.zeros((dev_count * capacity,), jnp.int32).at[position].set(obs_node)
    got_values, got_nodes = (
        lax.all_to_all(
            send_values.reshape(dev_count, capacity, realiz),
            ("sx", "sy"),
            split_axis=0,
            concat_axis=0,
            tiled=True,
        ),
        lax.all_to_all(
            send_nodes.reshape(dev_count, capacity),
            ("sx", "sy"),
            split_axis=0,
            concat_axis=0,
            tiled=True,
        ),
    )
    load = jax.ops.segment_sum(
        got_values.reshape(-1, realiz).astype(jnp.float32), got_nodes.reshape(-1), num_segments=size
    )
    rhs = assemble(load.T)
    weight = edge_weights(size)[None, :]
    basis = coarse_basis(size, count)
    schur_mat = schur[0, 0]
    inverse_mat = local_inverse[0, 0]

    def project(vec):
        return jnp.dot(weight * vec, basis, precision=hp).T

    def precond(vec, coarse_all):
        scaled = weight * vec
        part = jnp.dot(scaled.astype(jnp.bfloat16), inverse_mat, preferred_element_type=jnp.float32)
        solved = jnp.dot(coarse_inverse, coarse_all, precision=hp)
        correction = jnp.dot(solved.T, basis.T, precision=hp)
        return assemble(weight * (part + correction))

    def products(left, right):
        return lax.psum(jnp.sum(weight * left * right, axis=1), ("sx", "sy"))

    solution_field = jnp.zeros_like(rhs)
    residual = rhs
    coarse_resid = gather_coarse(project(residual))
    precon = precond(residual, coarse_resid)
    direction = precon
    rz_now = products(residual, precon)
    for step in range(ITERS):
        image = assemble(
            jnp.dot(direction.astype(jnp.bfloat16), schur_mat, preferred_element_type=jnp.float32)
        )
        curv_local = jnp.sum(weight * direction * image, axis=1)
        curv = lax.psum(curv_local, ("sx", "sy"))
        alpha = rz_now / curv
        solution_field = solution_field + alpha[:, None] * direction
        residual = residual - alpha[:, None] * image
        if step < ITERS - 1:
            coarse_resid = gather_coarse(project(residual))
            precon = precond(residual, coarse_resid)
            rz_next = products(residual, precon)
            direction = precon + (rz_next / rz_now)[:, None] * direction
            rz_now = rz_next
    return (solution_field[None, None], residual[None, None])


def solution(mesh):
    placed = (
        P(("sx", "sy"), None),
        P(("sx", "sy"), None),
        P(("sx", "sy")),
        P("sx", "sy", None, None),
        P("sx", "sy", None, None),
        P(("sx", "sy"), None),
    )
    return jax.shard_map(
        body,
        mesh=mesh,
        in_specs=placed,
        out_specs=(P("sx", "sy", None, None), P("sx", "sy", None, None)),
        check_vma=False,
    )
```

profile of v0, /device:TPU:1, one launch (start us, length us, event | category | flops | bytes accessed | tf_op | source)
XLA Modules:
  0.0 1432.0 jit_solution(6117860953516433841)
XLA Ops:
  5.6 11.5 all-to-all-start
  32.6 8.1 all-to-all-done.1
  60.7 7.6 collective-permute-done.3
  72.7 39.9 %all_gather.18 = f32[1024,64]{1,0:T(8,128)S(1)} all-gather(f32[8,64]{1,0:T(8,128)S(1)} %fusion.35), channel_id=1, replica_groups=mesh['sx'=16,'sy'=8] {'sx','sy'}, dimensions={0}, use_global_device_ids=true | all-gather | bytes 264192 | tf_op jit(solution)/shard_map/all_gather | solution.py:80
  136.0 7.7 collective-permute-done.7
  163.3 7.7 collective-permute-done.11
  172.5 69.8 %all-reduce = (f32[64]{0:T(128)S(1)}, f32[64]{0:T(128)S(1)}) all-reduce(f32[64]{0:T(128)S(1)} %get-tuple-element.3, f32[64]{0:T(128)S(1)} %get-tuple-element.2), channel_id=1, replica_groups=mesh['sx'=16,'sy'=8] {'sx','sy'}, use_global_device_ids=true, to_apply=%region_7.8 | all-reduce | flops 128 | bytes 1024 | tf_op jit(solution)/shard_map/psum | solution.py:136
  249.8 34.5 %all_gather.19 = f32[1024,64]{1,0:T(8,128)S(1)} all-gather(f32[8,64]{1,0:T(8,128)S(1)} %fusion.34), channel_id=1, replica_groups=mesh['sx'=16,'sy'=8] {'sx','sy'}, dimensions={0}, use_global_device_ids=true | all-gather | bytes 264192 | tf_op jit(solution)/shard_map/all_gather | solution.py:80
  302.5 7.7 collective-permute-done.15
  311.7 67.8 %psum.86 = f32[64]{0:T(128)S(1)} all-reduce(f32[64]{0:T(128)S(1)} %multiply_reduce_fusion.8), channel_id=1, replica_groups=mesh['sx'=16,'sy'=8] {'sx','sy'}, use_global_device_ids=true, to_apply=%region_11.12 | all-reduce | flops 64 | bytes 512 | tf_op jit(solution)/shard_map/psum | solution.py:136
  400.4 7.4 collective-permute-done.19
  409.6 68.1 %psum.87 = f32[64]{0:T(128)S(1)} all-reduce(f32[64]{0:T(128)S(1)} %multiply_reduce_fusion.7), channel_id=1, replica_groups=mesh['sx'=16,'sy'=8] {'sx','sy'}, use_global_device_ids=true, to_apply=%region_13.14 | all-reduce | flops 64 | bytes 512 | tf_op jit(solution)/shard_map/psum | solution.py:149
  485.2 34.6 %all_gather.20 = f32[1024,64]{1,0:T(8,128)S(1)} all-gather(f32[8,64]{1,0:T(8,128)S(1)} %fusion.33), channel_id=1, replica_groups=mesh['sx'=16,'sy'=8] {'sx','sy'}, dimensions={0}, use_global_device_ids=true | all-gather | bytes 264192 | tf_op jit(solution)/shard_map/all_gather | solution.py:80
  538.0 7.7 collective-permute-done.23
  547.9 68.0 %psum.88 = f32[64]{0:T(128)S(1)} all-reduce(f32[64]{0:T(128)S(1)} %multiply_reduce_fusion.6), channel_id=1, replica_groups=mesh['sx'=16,'sy'=8] {'sx','sy'}, use_global_device_ids=true, to_apply=%region_15.16 | all-reduce | flops 64 | bytes 512 | tf_op jit(solution)/shard_map/psum | solution.py:136
  637.8 7.3 collective-permute-done.27
  647.0 68.1 %psum.89 = f32[64]{0:T(128)S(1)} all-reduce(f32[64]{0:T(128)S(1)} %multiply_reduce_fusion.5), channel_id=1, replica_groups=mesh['sx'=16,'sy'=8] {'sx','sy'}, use_global_device_ids=true, to_apply=%region_17.18 | all-reduce | flops 64 | bytes 512 | tf_op jit(solution)/shard_map/psum | solution.py:149
  723.6 34.8 %all_gather.21 = f32[1024,64]{1,0:T(8,128)S(1)} all-gather(f32[8,64]{1,0:T(8,128)S(1)} %fusion.32), channel_id=1, replica_groups=mesh['sx'=16,'sy'=8] {'sx','sy'}, dimensions={0}, use_global_device_ids=true | all-gather | bytes 264192 | tf_op jit(solution)/shard_map/all_gather | solution.py:80
  776.6 7.7 collective-permute-done.31
  785.8 68.0 %psum.90 = f32[64]{0:T(128)S(1)} all-reduce(f32[64]{0:T(128)S(1)} %multiply_reduce_fusion.4), channel_id=1, replica_groups=mesh['sx'=16,'sy'=8] {'sx','sy'}, use_global_device_ids=true, to_apply=%region_19.20 | all-reduce | flops 64 | bytes 512 | tf_op jit(solution)/shard_map/psum | solution.py:136
  874.7 7.3 collective-permute-done.35
  883.9 68.1 %psum.91 = f32[64]{0:T(128)S(1)} all-reduce(f32[64]{0:T(128)S(1)} %multiply_reduce_fusion.3), channel_id=1, replica_groups=mesh['sx'=16,'sy'=8] {'sx','sy'}, use_global_device_ids=true, to_apply=%region_21.22 | all-reduce | flops 64 | bytes 512 | tf_op jit(solution)/shard_map/psum | solution.py:149
  959.4 34.5 %all_gather.22 = f32[1024,64]{1,0:T(8,128)S(1)} all-gather(f32[8,64]{1,0:T(8,128)S(1)} %fusion.31), channel_id=1, replica_groups=mesh['sx'=16,'sy'=8] {'sx','sy'}, dimensions={0}, use_global_device_ids=true | all-gather | bytes 264192 | tf_op jit(solution)/shard_map/all_gather | solution.py:80
  1012.2 7.7 collective-permute-done.39
  1022.2 68.0 %psum.92 = f32[64]{0:T(128)S(1)} all-reduce(f32[64]{0:T(128)S(1)} %multiply_reduce_fusion.2), channel_id=1, replica_groups=mesh['sx'=16,'sy'=8] {'sx','sy'}, use_global_device_ids=true, to_apply=%region_23.24 | all-reduce | flops 64 | bytes 512 | tf_op jit(solution)/shard_map/psum | solution.py:136
  1112.1 7.3 collective-permute-done.43
  1121.3 68.1 %psum.93 = f32[64]{0:T(128)S(1)} all-reduce(f32[64]{0:T(128)S(1)} %multiply_reduce_fusion.1), channel_id=1, replica_groups=mesh['sx'=16,'sy'=8] {'sx','sy'}, use_global_device_ids=true, to_apply=%region_25.26 | all-reduce | flops 64 | bytes 512 | tf_op jit(solution)/shard_map/psum | solution.py:149
  1196.8 34.6 %all_gather.23 = f32[1024,64]{1,0:T(8,128)S(1)} all-gather(f32[8,64]{1,0:T(8,128)S(1)} %fusion.30), channel_id=1, replica_groups=mesh['sx'=16,'sy'=8] {'sx','sy'}, dimensions={0}, use_global_device_ids=true | all-gather | bytes 264192 | tf_op jit(solution)/shard_map/all_gather | solution.py:80
  1249.6 7.7 collective-permute-done.47
  1258.8 68.0 %psum.94 = f32[64]{0:T(128)S(1)} all-reduce(f32[64]{0:T(128)S(1)} %multiply_reduce_fusion), channel_id=1, replica_groups=mesh['sx'=16,'sy'=8] {'sx','sy'}, use_global_device_ids=true, to_apply=%region_27.28 | all-reduce | flops 64 | bytes 512 | tf_op jit(solution)/shard_map/psum | solution.py:136
  1347.6 7.3 collective-permute-done.51
  1357.7 68.1 %psum.95 = f32[64]{0:T(128)S(1)} all-reduce(f32[64]{0:T(128)S(1)} %fusion.48), channel_id=1, replica_groups=mesh['sx'=16,'sy'=8] {'sx','sy'}, use_global_device_ids=true, to_apply=%region_29.30 | all-reduce | flops 64 | bytes 512 | tf_op jit(solution)/shard_map/psum | solution.py:149
  (316 shorter events, 348.6 us)
Async XLA Ops:
  5.6 21.0 %all-to-all-start = ((s32[128,1,4]{2,1,0:T(1,128)}), s32[128,1,4]{2,1,0:T(1,128)S(1)}, u32[]{:S(2)}, u32[]{:S(2)}) async-start(s32[128,1,4]{2,1,0:T(1,128)} %bitcast.7), calls=%async_computation | async-start | bytes 131072 | tf_op jit(solution)/shard_map/all_to_all | solution.py:108
  26.6 14.0 all-to-all-start.1
  53.7 14.6 %collective-permute-start.3 = (bf16[3,1,64,2048]{3,2,1,0:T(8,128)(2,1)S(1)}, bf16[3,1,64,2048]{3,2,1,0:T(8,128)(2,1)S(1)}, u32[]{:S(2)}, u32[]{:S(2)}) collective-permute-start(bf16[3,1,64,2048]{3,2,1,0:T(8,128)(2,1)S(1)} %pad_maximum_fusion), channel_id=1, source_target_pairs={{1,0},{2,1},{3,2},{4,3},{5,4},{6,5},{7,6},{9,8},{10,9},{11,10},{12... | collective-permute-start | bytes 2359304 | tf_op jit(solution)/shard_map/ppermute | solution.py:27
  57.6 11.9 collective-permute-start.2
  119.8 9.6 collective-permute-start.5
  130.4 13.3 collective-permute-start.7
  133.6 11.3 collective-permute-start.6
  156.1 15.0 %collective-permute-start.11 = (bf16[3,1,64,2048]{3,2,1,0:T(8,128)(2,1)S(1)}, bf16[3,1,64,2048]{3,2,1,0:T(8,128)(2,1)S(1)}, u32[]{:S(2)}, u32[]{:S(2)}) collective-permute-start(bf16[3,1,64,2048]{3,2,1,0:T(8,128)(2,1)S(1)} %pad_maximum_fusion.2), channel_id=1, source_target_pairs={{1,0},{2,1},{3,2},{4,3},{5,4},{6,5},{7,6},{9,8},{10,9},{11,10},{12... | collective-permute-start | bytes 2359304 | tf_op jit(solution)/shard_map/ppermute | solution.py:27
  158.0 14.2 collective-permute-start.10
  286.4 9.6 collective-permute-start.13
  297.0 13.3 collective-permute-start.15
  300.2 11.3 collective-permute-start.14
  394.3 13.5 collective-permute-start.19
  398.5 10.8 collective-permute-start.18
  521.8 9.6 collective-permute-start.21
  532.4 13.3 collective-permute-start.23
  535.6 11.3 collective-permute-start.22
  631.7 13.4 collective-permute-start.27
  635.9 10.8 collective-permute-start.26
  771.0 13.3 collective-permute-start.31
  774.2 11.3 collective-permute-start.30
  868.5 13.4 collective-permute-start.35
  872.8 10.8 collective-permute-start.34
  996.0 9.6 collective-permute-start.37
  1006.6 13.3 collective-permute-start.39
  1009.8 11.3 collective-permute-start.38
  1106.0 13.4 collective-permute-start.43
  1110.2 10.8 collective-permute-start.42
  1244.0 13.3 collective-permute-start.47
  1247.2 11.3 collective-permute-start.46
  1341.5 13.5 collective-permute-start.51
  1345.7 10.8 collective-permute-start.50
  (67 other events, 2812.2 us)
where the time goes:
time: 1440 us; the launch traced here: 1430 us
  blocking collectives  963 us (67%)
  waiting for transfers between devices  190 us (13%)
  starting transfers between devices  164 us (11%)
  matrix products  82.1 us (6%)
  other arithmetic  20.9 us (1%)
    psum x6, blocking collectives, products(): return lax.psum(jnp.sum(weight * left * right, axis=1), ('sx', 'sy'))  410 us
    psum x5, blocking collectives, body(): curv = lax.psum(curv_local, ('sx', 'sy'))  340 us
    all_gather x6, blocking collectives, gather_coarse(): return lax.all_gather(coarse_local, ('sx', 'sy'), axis=0, tiled=True)  213 us
    ppermute x26, waiting for transfers between devices, padded_2(): lax.ppermute(head, axis, [((i + 1) % count, i) for i in range(ends)])  146 us
    ppermute x26, starting transfers between devices, padded_2(): lax.ppermute(tail, axis, [(i, (i + 1) % count) for i in range(ends)])  84.9 us
    ppermute x26, starting transfers between devices, padded_2(): lax.ppermute(head, axis, [((i + 1) % count, i) for i in range(ends)])  62.8 us
    dot_general x6, matrix products, precond(): jnp.dot(scaled.astype(jnp.bfloat16), inverse_mat, preferred_element_type=...  29.9 us
    ppermute x26, waiting for transfers between devices, padded_2(): lax.ppermute(tail, axis, [(i, (i + 1) % count) for i in range(ends)])  29.5 us
  transfers between devices with their start and end apart: 54, of which 54 were waited for; matrix products, arithmetic and copies ran while one was open for 0% of the time, Pallas kernels for 0%

commit v1 on v0

--- a/solution.py
+++ b/solution.py
@@ -146,7 +146,7 @@
             jnp.dot(direction.astype(jnp.bfloat16), schur_mat, preferred_element_type=jnp.float32)
         )
         curv_local = jnp.sum(weight * direction * image, axis=1)
-        curv = lax.psum(curv_local, ("sx", "sy"))
+        curv = lax.psum(lax.psum(curv_local, "sx"), "sy")
         alpha = rz_now / curv
         solution_field = solution_field + alpha[:, None] * direction
         residual = residual - alpha[:, None] * image

time: 1440 us -> 1400 us (0.972)
  blocking collectives: 963 us -> 921 us
    psum x5 -> x12, blocking collectives: 340 us -> 310 us  [body(): curv = lax.psum(lax.psum(curv_local, 'sx'), 'sy')]
where the time goes in v1:
time: 1400 us; the launch traced here: 1390 us
  blocking collectives  921 us (66%)
  waiting for transfers between devices  191 us (14%)
  starting transfers between devices  163 us (12%)
  matrix products  82.1 us (6%)
  other arithmetic  20.9 us (1%)
    psum x6, blocking collectives, products(): return lax.psum(jnp.sum(weight * left * right, axis=1), ('sx', 'sy'))  406 us
    psum x12, blocking collectives, body(): curv = lax.psum(lax.psum(curv_local, 'sx'), 'sy')  310 us
    all_gather x6, blocking collectives, gather_coarse(): return lax.all_gather(coarse_local, ('sx', 'sy'), axis=0, tiled=True)  205 us
    ppermute x26, waiting for transfers between devices, padded_2(): lax.ppermute(head, axis, [((i + 1) % count, i) for i in range(ends)])  147 us
    ppermute x26, starting transfers between devices, padded_2(): lax.ppermute(tail, axis, [(i, (i + 1) % count) for i in range(ends)])  84.9 us
    ppermute x26, starting transfers between devices, padded_2(): lax.ppermute(head, axis, [((i + 1) % count, i) for i in range(ends)])  62.6 us
    dot_general x6, matrix products, precond(): jnp.dot(scaled.astype(jnp.bfloat16), inverse_mat, preferred_element_type=...  29.9 us
    ppermute x26, waiting for transfers between devices, padded_2(): lax.ppermute(tail, axis, [(i, (i + 1) % count) for i in range(ends)])  29.1 us
  transfers between devices with their start and end apart: 54, of which 54 were waited for; matrix products, arithmetic and copies ran while one was open for 0% of the time, Pallas kernels for 0%

profile of v1, /device:TPU:1, one launch (start us, length us, event | category | flops | bytes accessed | tf_op | source)
XLA Modules:
  0.0 1389.5 jit_solution(1930770638465826747)
XLA Ops:
  5.6 11.5 all-to-all-start
  32.6 8.1 all-to-all-done.1
  72.7 39.9 %all_gather.18 = f32[1024,64]{1,0:T(8,128)S(1)} all-gather(f32[8,64]{1,0:T(8,128)S(1)} %fusion.35), channel_id=1, replica_groups=mesh['sx'=16,'sy'=8] {'sx','sy'}, dimensions={0}, use_global_device_ids=true | all-gather | bytes 264192 | tf_op jit(solution)/shard_map/all_gather | solution.py:80
  136.0 7.7 collective-permute-done.7
  163.3 8.0 collective-permute-done.11
  172.5 32.7 %psum.127 = f32[64]{0:T(128)S(1)} all-reduce(f32[64]{0:T(128)S(1)} %get-tuple-element.2), channel_id=1, replica_groups=mesh['sx'=16,'sy'=8] {'sx'}, use_global_device_ids=true, to_apply=%region_9.10 | all-reduce | flops 64 | bytes 512 | tf_op jit(solution)/shard_map/psum | solution.py:149
  205.3 19.8 %psum.128 = f32[64]{0:T(128)S(1)} all-reduce(f32[64]{0:T(128)S(1)} %psum.127), channel_id=1, replica_groups=mesh['sx'=16,'sy'=8] {'sy'}, use_global_device_ids=true, to_apply=%region_10.11 | all-reduce | flops 64 | bytes 512 | tf_op jit(solution)/shard_map/psum | solution.py:149
  225.1 61.9 %psum.126 = f32[64]{0:T(128)S(1)} all-reduce(f32[64]{0:T(128)S(1)} %get-tuple-element.3), channel_id=1, replica_groups=mesh['sx'=16,'sy'=8] {'sx','sy'}, use_global_device_ids=true, to_apply=%region_7.8 | all-reduce | flops 64 | bytes 512 | tf_op jit(solution)/shard_map/psum | solution.py:136
  294.5 34.5 %all_gather.19 = f32[1024,64]{1,0:T(8,128)S(1)} all-gather(f32[8,64]{1,0:T(8,128)S(1)} %fusion.34), channel_id=1, replica_groups=mesh['sx'=16,'sy'=8] {'sx','sy'}, dimensions={0}, use_global_device_ids=true | all-gather | bytes 264192 | tf_op jit(solution)/shard_map/all_gather | solution.py:80
  347.2 7.7 collective-permute-done.15
  356.4 67.8 %psum.129 = f32[64]{0:T(128)S(1)} all-reduce(f32[64]{0:T(128)S(1)} %multiply_reduce_fusion.8), channel_id=1, replica_groups=mesh['sx'=16,'sy'=8] {'sx','sy'}, use_global_device_ids=true, to_apply=%region_12.13 | all-reduce | flops 64 | bytes 512 | tf_op jit(solution)/shard_map/psum | solution.py:136
  454.3 32.0 %psum.130 = f32[64]{0:T(128)S(1)} all-reduce(f32[64]{0:T(128)S(1)} %multiply_reduce_fusion.7), channel_id=1, replica_groups=mesh['sx'=16,'sy'=8] {'sx'}, use_global_device_ids=true, to_apply=%region_14.15 | all-reduce | flops 64 | bytes 512 | tf_op jit(solution)/shard_map/psum | solution.py:149
  486.3 19.5 %psum.131 = f32[64]{0:T(128)S(1)} all-reduce(f32[64]{0:T(128)S(1)} %psum.130), channel_id=1, replica_groups=mesh['sx'=16,'sy'=8] {'sy'}, use_global_device_ids=true, to_apply=%region_15.16 | all-reduce | flops 64 | bytes 512 | tf_op jit(solution)/shard_map/psum | solution.py:149
  513.1 32.6 %all_gather.20 = f32[1024,64]{1,0:T(8,128)S(1)} all-gather(f32[8,64]{1,0:T(8,128)S(1)} %fusion.33), channel_id=1, replica_groups=mesh['sx'=16,'sy'=8] {'sx','sy'}, dimensions={0}, use_global_device_ids=true | all-gather | bytes 264192 | tf_op jit(solution)/shard_map/all_gather | solution.py:80
  563.9 7.7 collective-permute-done.23
  573.9 69.1 %psum.132 = f32[64]{0:T(128)S(1)} all-reduce(f32[64]{0:T(128)S(1)} %multiply_reduce_fusion.6), channel_id=1, replica_groups=mesh['sx'=16,'sy'=8] {'sx','sy'}, use_global_device_ids=true, to_apply=%region_17.18 | all-reduce | flops 64 | bytes 512 | tf_op jit(solution)/shard_map/psum | solution.py:136
  674.0 32.0 %psum.133 = f32[64]{0:T(128)S(1)} all-reduce(f32[64]{0:T(128)S(1)} %multiply_reduce_fusion.5), channel_id=1, replica_groups=mesh['sx'=16,'sy'=8] {'sx'}, use_global_device_ids=true, to_apply=%region_19.20 | all-reduce | flops 64 | bytes 512 | tf_op jit(solution)/shard_map/psum | solution.py:149
  706.0 19.5 %psum.134 = f32[64]{0:T(128)S(1)} all-reduce(f32[64]{0:T(128)S(1)} %psum.133), channel_id=1, replica_groups=mesh['sx'=16,'sy'=8] {'sy'}, use_global_device_ids=true, to_apply=%region_20.21 | all-reduce | flops 64 | bytes 512 | tf_op jit(solution)/shard_map/psum | solution.py:149
  734.0 32.8 %all_gather.21 = f32[1024,64]{1,0:T(8,128)S(1)} all-gather(f32[8,64]{1,0:T(8,128)S(1)} %fusion.32), channel_id=1, replica_groups=mesh['sx'=16,'sy'=8] {'sx','sy'}, dimensions={0}, use_global_device_ids=true | all-gather | bytes 264192 | tf_op jit(solution)/shard_map/all_gather | solution.py:80
  785.0 7.7 collective-permute-done.31
  794.2 69.1 %psum.135 = f32[64]{0:T(128)S(1)} all-reduce(f32[64]{0:T(128)S(1)} %multiply_reduce_fusion.4), channel_id=1, replica_groups=mesh['sx'=16,'sy'=8] {'sx','sy'}, use_global_device_ids=true, to_apply=%region_22.23 | all-reduce | flops 64 | bytes 512 | tf_op jit(solution)/shard_map/psum | solution.py:136
  893.3 32.0 %psum.136 = f32[64]{0:T(128)S(1)} all-reduce(f32[64]{0:T(128)S(1)} %multiply_reduce_fusion.3), channel_id=1, replica_groups=mesh['sx'=16,'sy'=8] {'sx'}, use_global_device_ids=true, to_apply=%region_24.25 | all-reduce | flops 64 | bytes 512 | tf_op jit(solution)/shard_map/psum | solution.py:149
  925.3 19.5 %psum.137 = f32[64]{0:T(128)S(1)} all-reduce(f32[64]{0:T(128)S(1)} %psum.136), channel_id=1, replica_groups=mesh['sx'=16,'sy'=8] {'sy'}, use_global_device_ids=true, to_apply=%region_25.26 | all-reduce | flops 64 | bytes 512 | tf_op jit(solution)/shard_map/psum | solution.py:149
  952.2 32.5 %all_gather.22 = f32[1024,64]{1,0:T(8,128)S(1)} all-gather(f32[8,64]{1,0:T(8,128)S(1)} %fusion.31), channel_id=1, replica_groups=mesh['sx'=16,'sy'=8] {'sx','sy'}, dimensions={0}, use_global_device_ids=true | all-gather | bytes 264192 | tf_op jit(solution)/shard_map/all_gather | solution.py:80
  1002.9 7.7 collective-permute-done.39
  1012.9 69.1 %psum.138 = f32[64]{0:T(128)S(1)} all-reduce(f32[64]{0:T(128)S(1)} %multiply_reduce_fusion.2), channel_id=1, replica_groups=mesh['sx'=16,'sy'=8] {'sx','sy'}, use_global_device_ids=true, to_apply=%region_27.28 | all-reduce | flops 64 | bytes 512 | tf_op jit(solution)/shard_map/psum | solution.py:136
  1113.1 32.0 %psum.139 = f32[64]{0:T(128)S(1)} all-reduce(f32[64]{0:T(128)S(1)} %multiply_reduce_fusion.1), channel_id=1, replica_groups=mesh['sx'=16,'sy'=8] {'sx'}, use_global_device_ids=true, to_apply=%region_29.30 | all-reduce | flops 64 | bytes 512 | tf_op jit(solution)/shard_map/psum | solution.py:149
  1145.1 19.5 %psum.140 = f32[64]{0:T(128)S(1)} all-reduce(f32[64]{0:T(128)S(1)} %psum.139), channel_id=1, replica_groups=mesh['sx'=16,'sy'=8] {'sy'}, use_global_device_ids=true, to_apply=%region_30.31 | all-reduce | flops 64 | bytes 512 | tf_op jit(solution)/shard_map/psum | solution.py:149
  1172.0 32.6 %all_gather.23 = f32[1024,64]{1,0:T(8,128)S(1)} all-gather(f32[8,64]{1,0:T(8,128)S(1)} %fusion.30), channel_id=1, replica_groups=mesh['sx'=16,'sy'=8] {'sx','sy'}, dimensions={0}, use_global_device_ids=true | all-gather | bytes 264192 | tf_op jit(solution)/shard_map/all_gather | solution.py:80
  1232.0 69.1 %psum.141 = f32[64]{0:T(128)S(1)} all-reduce(f32[64]{0:T(128)S(1)} %multiply_reduce_fusion), channel_id=1, replica_groups=mesh['sx'=16,'sy'=8] {'sx','sy'}, use_global_device_ids=true, to_apply=%region_32.33 | all-reduce | flops 64 | bytes 512 | tf_op jit(solution)/shard_map/psum | solution.py:136
  1331.9 32.0 %psum.142 = f32[64]{0:T(128)S(1)} all-reduce(f32[64]{0:T(128)S(1)} %fusion.48), channel_id=1, replica_groups=mesh['sx'=16,'sy'=8] {'sx'}, use_global_device_ids=true, to_apply=%region_34.35 | all-reduce | flops 64 | bytes 512 | tf_op jit(solution)/shard_map/psum | solution.py:149
  1363.9 19.5 %psum.143 = f32[64]{0:T(128)S(1)} all-reduce(f32[64]{0:T(128)S(1)} %psum.142), channel_id=1, replica_groups=mesh['sx'=16,'sy'=8] {'sy'}, use_global_device_ids=true, to_apply=%region_35.36 | all-reduce | flops 64 | bytes 512 | tf_op jit(solution)/shard_map/psum | solution.py:149
  (323 shorter events, 400.2 us)
Async XLA Ops:
  5.6 21.0 %all-to-all-start = ((s32[128,1,4]{2,1,0:T(1,128)}), s32[128,1,4]{2,1,0:T(1,128)S(1)}, u32[]{:S(2)}, u32[]{:S(2)}) async-start(s32[128,1,4]{2,1,0:T(1,128)} %bitcast.7), calls=%async_computation | async-start | bytes 131072 | tf_op jit(solution)/shard_map/all_to_all | solution.py:108
  26.6 14.0 %all-to-all-start.1 = ((bf16[128,2,128]{2,1,0:T(2,128)(2,1)}), bf16[128,2,128]{2,1,0:T(2,128)(2,1)S(1)}, u32[]{:S(2)}, u32[]{:S(2)}) async-start(bf16[128,2,128]{2,1,0:T(2,128)(2,1)} %reshape.1414), calls=%async_computation.1 | async-start | bytes 131072 | tf_op jit(solution)/shard_map/all_to_all | solution.py:101
  53.7 14.6 %collective-permute-start.3 = (bf16[3,1,64,2048]{3,2,1,0:T(8,128)(2,1)S(1)}, bf16[3,1,64,2048]{3,2,1,0:T(8,128)(2,1)S(1)}, u32[]{:S(2)}, u32[]{:S(2)}) collective-permute-start(bf16[3,1,64,2048]{3,2,1,0:T(8,128)(2,1)S(1)} %pad_maximum_fusion), channel_id=1, source_target_pairs={{1,0},{2,1},{3,2},{4,3},{5,4},{6,5},{7,6},{9,8},{10,9},{11,10},{12... | collective-permute-start | bytes 2359304 | tf_op jit(solution)/shard_map/ppermute | solution.py:27
  57.6 11.9 collective-permute-start.2
  119.8 9.6 collective-permute-start.5
  130.4 13.3 collective-permute-start.7
  133.6 11.3 collective-permute-start.6
  156.1 15.3 %collective-permute-start.11 = (bf16[3,1,64,2048]{3,2,1,0:T(8,128)(2,1)S(1)}, bf16[3,1,64,2048]{3,2,1,0:T(8,128)(2,1)S(1)}, u32[]{:S(2)}, u32[]{:S(2)}) collective-permute-start(bf16[3,1,64,2048]{3,2,1,0:T(8,128)(2,1)S(1)} %pad_maximum_fusion.2), channel_id=1, source_target_pairs={{1,0},{2,1},{3,2},{4,3},{5,4},{6,5},{7,6},{9,8},{10,9},{11,10},{12... | collective-permute-start | bytes 2359304 | tf_op jit(solution)/shard_map/ppermute | solution.py:27
  158.0 14.2 %collective-permute-start.10 = (bf16[3,1,64,2048]{3,2,1,0:T(8,128)(2,1)S(1)}, bf16[3,1,64,2048]{3,2,1,0:T(8,128)(2,1)S(1)}, u32[]{:S(2)}, u32[]{:S(2)}) collective-permute-start(bf16[3,1,64,2048]{3,2,1,0:T(8,128)(2,1)S(1)} %pad_maximum_fusion.2), channel_id=1, source_target_pairs={{0,1},{1,2},{2,3},{3,4},{4,5},{5,6},{6,7},{8,9},{9,10},{10,11},{11... | collective-permute-start | bytes 2359304 | tf_op jit(solution)/shard_map/ppermute | solution.py:25
  331.0 9.6 collective-permute-start.13
  341.6 13.3 collective-permute-start.15
  344.8 11.3 collective-permute-start.14
  439.1 13.3 collective-permute-start.19
  443.2 10.8 collective-permute-start.18
  547.8 9.6 collective-permute-start.21
  558.4 13.3 collective-permute-start.23
  561.6 11.3 collective-permute-start.22
  658.7 13.4 collective-permute-start.27
  662.9 10.8 collective-permute-start.26
  768.8 9.6 collective-permute-start.29
  779.4 13.3 collective-permute-start.31
  782.6 11.3 collective-permute-start.30
  878.0 13.4 collective-permute-start.35
  882.2 10.8 collective-permute-start.34
  997.4 13.3 collective-permute-start.39
  1000.6 11.3 collective-permute-start.38
  1097.8 13.4 collective-permute-start.43
  1102.0 10.8 collective-permute-start.42
  1217.2 13.3 collective-permute-start.47
  1220.4 11.3 collective-permute-start.46
  1315.7 13.5 collective-permute-start.51
  1319.9 10.8 collective-permute-start.50
  (67 other events, 2574.9 us)
